TPU v7x, 32 devices: a whole 2x2x4 slice. The times are simulated.
32 devices in a mesh: beam: 1, freq: 32 (over z, y, x, core), tm: 1.
Axes of the slice: x: 2, y: 2, z: 4, core: 2. Of those that a mesh axis runs over, the one named last changes fastest.
Arguments:
- data: bfloat16 [4096, 640], P(('beam', 'freq'), 'tm'), may hold values from -1000 to 1000
- chan_delay: int32 [64, 4096], P(None, 'freq'), may hold values from 0 to 40, as said below
- sub_delay: int32 [2048, 64], P('freq'), may hold values from 0 to 24, as said below
- widths: int32 [16], replicated, may hold values from 1 to 256, as said below
Outputs:
- snr: float32 [2048, 16], P(('beam', 'freq'))
Inputs may be any that keep to these rules, and one draw needn't show every extreme that they name: chan_delay[s, c] is never smaller for a larger trial s; the value 40 is reached. sub_delay[d, b] is never smaller for a larger trial d; the value 24 is reached. The widths are distinct and include 1 and 256.
All inputs are finite; a program needn't handle non-finite values.
Results may differ from a plain program's by a relative error of at most 0.0014.
Values may be sent and summed in bfloat16 or wider, within the bound.
A program may use at most 64 MiB of HBM per device.

v0:
```python
import jax
import jax.numpy as jnp
from jax import lax
from jax.sharding import PartitionSpec as P

NSUB = 64
NSDM = 64
WMAX = 256
CPS = 64
DPS = 32
D1MAX = 40
D2MAX = 24


def passed_along(value, axis, steps):
    count = lax.axis_size(axis)
    initial, last = (max(0, -steps), min(count, count - steps))
    return lax.ppermute(value, axis, [(source, source + steps) for source in range(initial, last)])


def shifted_sum(source, delays, length, largest):
    band_count = source.shape[0]
    trial_count = delays.shape[1]
    start_total = jnp.zeros((band_count, trial_count, length), jnp.float32)

    def add_shifts(step_index, running_total):
        for within in range(2):
            offset = 2 * step_index + within
            window = lax.dynamic_slice_in_dim(source, offset, length, 2)
            selector = (delays == offset).astype(jnp.bfloat16)
            running_total = running_total + jnp.einsum(
                "bsm,bmt->bst", selector, window, preferred_element_type=jnp.float32
            )
        return running_total

    return lax.fori_loop(0, (largest + 2) // 2, add_shifts, start_total)


def form_subbands(extended, chan_delay, length):
    band_count = extended.shape[0] // CPS
    channel_slabs = extended.reshape(band_count, CPS, extended.shape[1])
    trial_delays = chan_delay.reshape(NSDM, band_count, CPS).transpose(1, 0, 2)
    return shifted_sum(channel_slabs, trial_delays, length, D1MAX).astype(jnp.bfloat16)


def peak_scores(normed, widths, span):
    running = jnp.concatenate(
        [jnp.zeros((normed.shape[0], 1), normed.dtype), jnp.cumsum(normed, axis=1)], axis=1
    )

    def one_width(width):
        upper = lax.dynamic_slice_in_dim(running, width, span, 1)
        return jnp.max((upper - running[:, :span]) / jnp.sqrt(width.astype(jnp.float32)), axis=1)

    return lax.map(one_width, widths).T


def on_device(data, chan_delay, sub_delay, widths):
    block_len = data.shape[1]
    total_len = block_len * lax.axis_size("tm")
    edge_rows = passed_along(data[:, :D1MAX], "tm", -1)
    extended = jnp.concatenate([data, edge_rows], axis=1)
    subband = form_subbands(extended, chan_delay, block_len)
    regrouped = lax.all_to_all(subband, "freq", split_axis=1, concat_axis=0, tiled=True)
    later = passed_along(regrouped[:, :, : D2MAX + WMAX], "tm", -1)
    regrouped = jnp.concatenate([regrouped, later], axis=2)
    dm_len = block_len + WMAX
    local_trials = regrouped.shape[1]
    grouped = sub_delay.reshape(local_trials, DPS, NSUB)
    by_trial = jnp.transpose(regrouped, (1, 0, 2))
    series = shifted_sum(by_trial, grouped, dm_len, D2MAX)
    series = series.reshape(local_trials * DPS, dm_len)
    inside = series[:, :block_len]
    totals = lax.psum(jnp.sum(inside, axis=1), "tm")
    average = totals / total_len
    centred = lax.psum(jnp.sum((inside - average[:, None]) ** 2, axis=1), "tm")
    spread = centred / total_len
    deviation = jnp.sqrt(spread + 1e-05)
    normed = (series - average[:, None]) / deviation[:, None]
    local_peaks = peak_scores(normed, widths, block_len)
    return lax.pmax(local_peaks, "tm")


def solution(mesh):
    in_specs = (P(("beam", "freq"), "tm"), P(None, "freq"), P("freq", None), P())
    out_specs = P(("beam", "freq"), None)
    return jax.shard_map(
        on_device, mesh=mesh, in_specs=in_specs, out_specs=out_specs, check_vma=False
    )
```

profile of v0, /device:TPU:0, one launch (start us, length us, event | category | flops | bytes accessed | tf_op | source)
XLA Modules:
  0.0 113.1 jit_solution(8462801548442391960)
XLA Ops:
  0.0 0.8 slice.18
  0.8 0.6 collective-permute-start
  1.5 0.9 reshape.42
  2.4 11.9 %while.43 = (s32[]{:T(128)}, f32[2,64,640]{2,1,0:T(8,128)S(1)}, s32[2,64,64]{2,1,0:T(8,128)S(1)}, bf16[2,64,680]{2,1,0:T(8,128)(2,1)S(1)}, s32[]{:T(128)}, /*index=5*/s32[]{:T(128)}, s32[]{:T(128)}, s32[]{:T(128)}, s32[]{:T(128)}) while((s32[]{:T(128)}, f32[2,64,640]{2,1,0:T(8,128)S(1)}, s32[2,64,64]{2,1,0:T(8,128)S(1)}, ...), condition=%wide.region_1.0_spmd.clone, body=%wide.region_0.0_spmd.clone.sunk | while | flops 21233676 | bytes 1769683 | solution.py:36
  2.4 0.3 convolution_add_fusion.8
  2.7 0.3 convolution_add_fusion.9
  3.6 0.3 convolution_add_fusion.8
  4.1 0.3 convolution_add_fusion.8
  4.4 0.3 convolution_add_fusion.9
  4.7 0.3 convolution_add_fusion.8
  5.3 0.3 convolution_add_fusion.8
  5.8 0.3 convolution_add_fusion.8
  6.1 0.3 convolution_add_fusion.9
  6.4 0.3 convolution_add_fusion.8
  7.0 0.3 convolution_add_fusion.8
  7.5 0.3 convolution_add_fusion.8
  7.8 0.3 convolution_add_fusion.9
  8.7 0.3 convolution_add_fusion.8
  9.2 0.3 convolution_add_fusion.8
  9.5 0.3 convolution_add_fusion.9
  9.8 0.3 convolution_add_fusion.8
  11.2 0.3 convolution_add_fusion.9
  12.1 0.3 convolution_add_fusion.8
  12.9 0.3 convolution_add_fusion.9
  13.8 0.3 convolution_add_fusion.8
  14.6 15.8 %all_to_all.18 = bf16[2,64,640]{2,0,1:T(2,128)(2,1)S(1)} all-to-all(bf16[2,64,640]{2,0,1:T(2,128)(2,1)S(1)} %copy.19), channel_id=1, replica_groups=mesh['beam'=1,'freq'=32,'tm'=1] {'freq'}, dimensions={1} | all-to-all | bytes 327680 | tf_op jit(solution)/shard_map/all_to_all | solution.py:64
  30.6 0.7 collective-permute-start.1
  31.3 0.7 copy-done
  32.0 7.4 %while.44 = (s32[]{:T(128)}, f32[2,32,896]{2,1,0:T(8,128)S(1)}, s32[2,32,64]{2,1,0:T(8,128)S(1)}, bf16[2,64,920]{2,1,0:T(8,128)(2,1)S(1)}, s32[]{:T(128)}, /*index=5*/s32[]{:T(128)}, s32[]{:T(128)}, s32[]{:T(128)}, s32[]{:T(128)}) while((s32[]{:T(128)}, f32[2,32,896]{2,1,0:T(8,128)S(1)}, s32[2,32,64]{2,1,0:T(8,128)S(1)}, ...), condition=%wide.region_3.0_spmd.clone, body=%wide.region_2.0_spmd.clone.sunk | while | flops 14860299 | bytes 1442003 | solution.py:36
  40.0 2.1 %reduce-window.6 = f32[64,7,128]{2,0,1:T(8,128)S(1)} reduce-window(f32[64,7,128]{2,0,1:T(8,128)S(1)} %copy.14, f32[]{:T(128)} %constant.116.clone.1), window={size=1x1x128 pad=0_0x0_0x127_0}, to_apply=%region_6.0 | reduce-window | flops 7282688 | bytes 458756 | tf_op jit(solution)/shard_map/reduce-window
  42.7 0.5 copy-done.2
  43.2 69.9 %while.42 = (s32[]{:T(128)}, f32[16,64]{1,0:T(8,128)}, s32[16]{0:T(128)S(1)}, f32[64,897]{1,0:T(8,128)S(1)}, s32[]{:T(128)}, /*index=5*/s32[]{:T(128)}, s32[]{:T(128)}) while((s32[]{:T(128)}, f32[16,64]{1,0:T(8,128)}, s32[16]{0:T(128)S(1)}, f32[64,897]{1,0:T(8,128)S(1)}, s32[]{:T(128)}, /*index=5*/s32[]{:T(128)}, s32[]{:T(128)}) %tuple.101), condition=%wide.region_10.11_spmd, body=%wide.region_8.10_spmd.sunk | while | flops 122822 | bytes 328599 | solution.py:55
  43.2 0.6 dynamic_slice.69
  46.3 1.3 %dynamic_update_slice.5 = f32[16,64]{1,0:T(8,128)} dynamic-update-slice(f32[16,64]{1,0:T(8,128)} %get-tuple-element.449, f32[1,64]{1,0:T(1,128)S(1)} %bitcast.30, s32[]{:T(128)} %get-tuple-element.448, s32[]{:T(128)} %constant.115.clone.1..sunk) | dynamic-update-slice | bytes 516 | tf_op jit(solution)/shard_map/while/body/jit(dynamic_update_index_in_dim)/dynamic_update_slice | solution.py:55
  47.6 0.6 dynamic_slice.69
  50.6 1.3 %dynamic_update_slice.5 = f32[16,64]{1,0:T(8,128)} dynamic-update-slice(f32[16,64]{1,0:T(8,128)} %get-tuple-element.449, f32[1,64]{1,0:T(1,128)S(1)} %bitcast.30, s32[]{:T(128)} %get-tuple-element.448, s32[]{:T(128)} %constant.115.clone.1..sunk) | dynamic-update-slice | bytes 516 | tf_op jit(solution)/shard_map/while/body/jit(dynamic_update_index_in_dim)/dynamic_update_slice | solution.py:55
  51.9 0.6 dynamic_slice.69
  55.0 1.3 %dynamic_update_slice.5 = f32[16,64]{1,0:T(8,128)} dynamic-update-slice(f32[16,64]{1,0:T(8,128)} %get-tuple-element.449, f32[1,64]{1,0:T(1,128)S(1)} %bitcast.30, s32[]{:T(128)} %get-tuple-element.448, s32[]{:T(128)} %constant.115.clone.1..sunk) | dynamic-update-slice | bytes 516 | tf_op jit(solution)/shard_map/while/body/jit(dynamic_update_index_in_dim)/dynamic_update_slice | solution.py:55
  56.3 0.6 dynamic_slice.69
  59.4 1.3 %dynamic_update_slice.5 = f32[16,64]{1,0:T(8,128)} dynamic-update-slice(f32[16,64]{1,0:T(8,128)} %get-tuple-element.449, f32[1,64]{1,0:T(1,128)S(1)} %bitcast.30, s32[]{:T(128)} %get-tuple-element.448, s32[]{:T(128)} %constant.115.clone.1..sunk) | dynamic-update-slice | bytes 516 | tf_op jit(solution)/shard_map/while/body/jit(dynamic_update_index_in_dim)/dynamic_update_slice | solution.py:55
  60.7 0.6 dynamic_slice.69
  63.7 1.3 %dynamic_update_slice.5 = f32[16,64]{1,0:T(8,128)} dynamic-update-slice(f32[16,64]{1,0:T(8,128)} %get-tuple-element.449, f32[1,64]{1,0:T(1,128)S(1)} %bitcast.30, s32[]{:T(128)} %get-tuple-element.448, s32[]{:T(128)} %constant.115.clone.1..sunk) | dynamic-update-slice | bytes 516 | tf_op jit(solution)/shard_map/while/body/jit(dynamic_update_index_in_dim)/dynamic_update_slice | solution.py:55
  65.0 0.6 dynamic_slice.69
  68.1 1.3 %dynamic_update_slice.5 = f32[16,64]{1,0:T(8,128)} dynamic-update-slice(f32[16,64]{1,0:T(8,128)} %get-tuple-element.449, f32[1,64]{1,0:T(1,128)S(1)} %bitcast.30, s32[]{:T(128)} %get-tuple-element.448, s32[]{:T(128)} %constant.115.clone.1..sunk) | dynamic-update-slice | bytes 516 | tf_op jit(solution)/shard_map/while/body/jit(dynamic_update_index_in_dim)/dynamic_update_slice | solution.py:55
  69.4 0.6 dynamic_slice.69
  72.5 1.3 %dynamic_update_slice.5 = f32[16,64]{1,0:T(8,128)} dynamic-update-slice(f32[16,64]{1,0:T(8,128)} %get-tuple-element.449, f32[1,64]{1,0:T(1,128)S(1)} %bitcast.30, s32[]{:T(128)} %get-tuple-element.448, s32[]{:T(128)} %constant.115.clone.1..sunk) | dynamic-update-slice | bytes 516 | tf_op jit(solution)/shard_map/while/body/jit(dynamic_update_index_in_dim)/dynamic_update_slice | solution.py:55
  73.8 0.6 dynamic_slice.69
  76.9 1.3 %dynamic_update_slice.5 = f32[16,64]{1,0:T(8,128)} dynamic-update-slice(f32[16,64]{1,0:T(8,128)} %get-tuple-element.449, f32[1,64]{1,0:T(1,128)S(1)} %bitcast.30, s32[]{:T(128)} %get-tuple-element.448, s32[]{:T(128)} %constant.115.clone.1..sunk) | dynamic-update-slice | bytes 516 | tf_op jit(solution)/shard_map/while/body/jit(dynamic_update_index_in_dim)/dynamic_update_slice | solution.py:55
  78.2 0.6 dynamic_slice.69
  81.2 1.3 %dynamic_update_slice.5 = f32[16,64]{1,0:T(8,128)} dynamic-update-slice(f32[16,64]{1,0:T(8,128)} %get-tuple-element.449, f32[1,64]{1,0:T(1,128)S(1)} %bitcast.30, s32[]{:T(128)} %get-tuple-element.448, s32[]{:T(128)} %constant.115.clone.1..sunk) | dynamic-update-slice | bytes 516 | tf_op jit(solution)/shard_map/while/body/jit(dynamic_update_index_in_dim)/dynamic_update_slice | solution.py:55
  82.5 0.6 dynamic_slice.69
  85.6 1.3 %dynamic_update_slice.5 = f32[16,64]{1,0:T(8,128)} dynamic-update-slice(f32[16,64]{1,0:T(8,128)} %get-tuple-element.449, f32[1,64]{1,0:T(1,128)S(1)} %bitcast.30, s32[]{:T(128)} %get-tuple-element.448, s32[]{:T(128)} %constant.115.clone.1..sunk) | dynamic-update-slice | bytes 516 | tf_op jit(solution)/shard_map/while/body/jit(dynamic_update_index_in_dim)/dynamic_update_slice | solution.py:55
  86.9 0.6 dynamic_slice.69
  90.0 1.3 %dynamic_update_slice.5 = f32[16,64]{1,0:T(8,128)} dynamic-update-slice(f32[16,64]{1,0:T(8,128)} %get-tuple-element.449, f32[1,64]{1,0:T(1,128)S(1)} %bitcast.30, s32[]{:T(128)} %get-tuple-element.448, s32[]{:T(128)} %constant.115.clone.1..sunk) | dynamic-update-slice | bytes 516 | tf_op jit(solution)/shard_map/while/body/jit(dynamic_update_index_in_dim)/dynamic_update_slice | solution.py:55
  91.3 0.6 dynamic_slice.69
  94.3 1.3 %dynamic_update_slice.5 = f32[16,64]{1,0:T(8,128)} dynamic-update-slice(f32[16,64]{1,0:T(8,128)} %get-tuple-element.449, f32[1,64]{1,0:T(1,128)S(1)} %bitcast.30, s32[]{:T(128)} %get-tuple-element.448, s32[]{:T(128)} %constant.115.clone.1..sunk) | dynamic-update-slice | bytes 516 | tf_op jit(solution)/shard_map/while/body/jit(dynamic_update_index_in_dim)/dynamic_update_slice | solution.py:55
  95.7 0.6 dynamic_slice.69
  98.7 1.3 %dynamic_update_slice.5 = f32[16,64]{1,0:T(8,128)} dynamic-update-slice(f32[16,64]{1,0:T(8,128)} %get-tuple-element.449, f32[1,64]{1,0:T(1,128)S(1)} %bitcast.30, s32[]{:T(128)} %get-tuple-element.448, s32[]{:T(128)} %constant.115.clone.1..sunk) | dynamic-update-slice | bytes 516 | tf_op jit(solution)/shard_map/while/body/jit(dynamic_update_index_in_dim)/dynamic_update_slice | solution.py:55
  100.0 0.6 dynamic_slice.69
  103.1 1.3 %dynamic_update_slice.5 = f32[16,64]{1,0:T(8,128)} dynamic-update-slice(f32[16,64]{1,0:T(8,128)} %get-tuple-element.449, f32[1,64]{1,0:T(1,128)S(1)} %bitcast.30, s32[]{:T(128)} %get-tuple-element.448, s32[]{:T(128)} %constant.115.clone.1..sunk) | dynamic-update-slice | bytes 516 | tf_op jit(solution)/shard_map/while/body/jit(dynamic_update_index_in_dim)/dynamic_update_slice | solution.py:55
  104.4 0.6 dynamic_slice.69
  107.5 1.3 %dynamic_update_slice.5 = f32[16,64]{1,0:T(8,128)} dynamic-update-slice(f32[16,64]{1,0:T(8,128)} %get-tuple-element.449, f32[1,64]{1,0:T(1,128)S(1)} %bitcast.30, s32[]{:T(128)} %get-tuple-element.448, s32[]{:T(128)} %constant.115.clone.1..sunk) | dynamic-update-slice | bytes 516 | tf_op jit(solution)/shard_map/while/body/jit(dynamic_update_index_in_dim)/dynamic_update_slice | solution.py:55
  108.8 0.6 dynamic_slice.69
  111.8 1.3 %dynamic_update_slice.5 = f32[16,64]{1,0:T(8,128)} dynamic-update-slice(f32[16,64]{1,0:T(8,128)} %get-tuple-element.449, f32[1,64]{1,0:T(1,128)S(1)} %bitcast.30, s32[]{:T(128)} %get-tuple-element.448, s32[]{:T(128)} %constant.115.clone.1..sunk) | dynamic-update-slice | bytes 516 | tf_op jit(solution)/shard_map/while/body/jit(dynamic_update_index_in_dim)/dynamic_update_slice | solution.py:55
  (90 shorter events, 17.4 us)
Async XLA Ops:
  0.0 2.4 %copy-start.1 = (bf16[128,640]{1,0:T(8,128)(2,1)S(1)}, bf16[128,640]{1,0:T(8,128)(2,1)}, u32[]{:S(2)}) copy-start(bf16[128,640]{1,0:T(8,128)(2,1)} %param.10) | copy-start | bytes 491524
  0.8 1.5 %collective-permute-start = (bf16[128,40]{1,0:T(8,128)(2,1)S(1)}, bf16[128,40]{1,0:T(8,128)(2,1)S(1)}, u32[]{:S(2)}, u32[]{:S(2)}) collective-permute-start(bf16[128,40]{1,0:T(8,128)(2,1)S(1)} %slice.18), channel_id=1, source_target_pairs={} | collective-permute-start | bytes 30728 | tf_op jit(solution)/shard_map/ppermute | solution.py:18
  30.6 0.7 collective-permute-start.1
  31.3 0.8 copy-start
  42.5 0.7 copy-start.2
where the time goes:
time: 114 us; the launch traced here: 113 us
  loops' own time  37.8 us (33%)
  local copies, waits for them, and re-layouts  33.8 us (30%)
  matrix products  18 us (16%)
  blocking collectives  15.8 us (14%)
  other arithmetic  6.21 us (5%)
  starting transfers between devices  1.3 us (1%)
    another operation x1, loops' own time, peak_scores(): return lax.map(one_width, widths).T  36.5 us
    dynamic_update_slice x16, local copies, waits for them, and re-layouts, peak_scores(): return lax.map(one_width, widths).T  20.8 us
    dot_general x68, matrix products, add_shifts(): jnp.einsum('bsm,bmt->bst', selector, window, preferred_element_type=jnp.f...  18 us
    all_to_all x1, blocking collectives, on_device(): lax.all_to_all(subband, 'freq', split_axis=1, concat_axis=0, tiled=True)  15.8 us
    dynamic_slice x16, local copies, waits for them, and re-layouts, peak_scores(): return lax.map(one_width, widths).T  9.2 us
    reduce_max x16, other arithmetic, one_width(): jnp.max((upper - running[:, :span]) / jnp.sqrt(width.astype(jnp.float32))...  3.39 us
  transfers between devices with their start and end apart: 2, of which 0 were waited for; matrix products, arithmetic and copies ran while one was open for 1% of the time, Pallas kernels for 0%

commit v1 on v0

--- a/solution.py
+++ b/solution.py
@@ -1,6 +1,10 @@
+import functools
+
 import jax
 import jax.numpy as jnp
 from jax import lax
+from jax.experimental import pallas as pl
+from jax.experimental.pallas import tpu as pltpu
 from jax.sharding import PartitionSpec as P
 
 NSUB = 64
@@ -81,9 +85,172 @@
     return lax.pmax(local_peaks, "tm")
 
 
+def fused_kernel(peers, block_len, data_ref, chan_ref, sub_ref, width_ref, out_ref,
+                 times, shifted, select, product, outgoing, incoming,
+                 running, send_sem, recv_sem, own_sem):
+    me = lax.axis_index("freq")
+    rows = data_ref.shape[0]
+    bands = rows // CPS
+    own_trials = NSDM // peers
+    dms = sub_ref.shape[0]
+    lanes = 2 * dms
+    group = bands * own_trials
+    f32, bf16 = jnp.float32, jnp.bfloat16
+
+    barrier = pltpu.get_barrier_semaphore()
+
+    def greet(step, carry):
+        pl.semaphore_signal(barrier, inc=1, device_id={"freq": lax.rem(me + step, peers)},
+                            device_id_type=pl.DeviceIdType.MESH)
+        return carry
+
+    lax.fori_loop(1, peers, greet, 0)
+
+    def iota(shape, axis):
+        return lax.broadcasted_iota(jnp.int32, shape, axis)
+
+    def expand(delay_of, largest, width):
+        for low in range(8):
+            for high in range(largest // 8 + 1):
+                if 8 * high + low > largest:
+                    block = jnp.zeros((rows, width), bf16)
+                else:
+                    block = jnp.where(delay_of == float(8 * high + low), 1.0, 0.0).astype(bf16)
+                select[low * rows:(low + 1) * rows, high * width:(high + 1) * width] = block
+
+    def shifted_total(largest, width):
+        highs = largest // 8 + 1
+        length = block_len + 8 * highs
+        for low in range(8):
+            shifted[0:length, low * rows:(low + 1) * rows] = times[low:low + length, :].astype(bf16)
+        for start in range(0, length, 128):
+            stop = min(start + 128, length)
+            product[start:stop, 0:highs * width] = jnp.dot(
+                shifted[start:stop, :], select[:, 0:highs * width], preferred_element_type=f32)
+        total = product[0:block_len, 0:width]
+        for high in range(1, highs):
+            total = total + product[8 * high:8 * high + block_len, high * width:(high + 1) * width]
+        return total
+
+    out_cols = NSDM * bands
+    spread = (iota((NSDM, out_cols), 1) // bands == iota((NSDM, out_cols), 0)).astype(bf16)
+    chan = chan_ref[...].astype(f32).astype(bf16)
+    delay = lax.dot_general(chan, spread, (((0,), (0,)), ((), ())), preferred_element_type=f32)
+    same = iota((rows, out_cols), 0) // CPS == iota((rows, out_cols), 1) % bands
+    expand(jnp.where(same, delay, -1.0), D1MAX, out_cols)
+    for start in range(0, block_len, 128):
+        times[start:start + 128, :] = data_ref[:, start:start + 128].astype(f32).T
+    times[block_len:, :] = jnp.zeros((times.shape[0] - block_len, rows), f32)
+    subband = shifted_total(D1MAX, out_cols)
+    for start in range(0, block_len, 128):
+        block = subband[start:start + 128, :].T.astype(bf16)
+        outgoing[:, :, start:start + 128] = block.reshape(peers, group, 128)
+
+    pl.semaphore_wait(barrier, peers - 1)
+
+    def sending(step):
+        return pltpu.make_async_remote_copy(
+            src_ref=outgoing.at[lax.rem(me + step, peers)], dst_ref=incoming.at[me],
+            send_sem=send_sem.at[step], recv_sem=recv_sem.at[step],
+            device_id={"freq": lax.rem(me + step, peers)}, device_id_type=pl.DeviceIdType.MESH)
+
+    def start_one(step, carry):
+        sending(step).start()
+        return carry
+
+    lax.fori_loop(1, peers, start_one, 0)
+    own = pltpu.make_async_copy(outgoing.at[me], incoming.at[me], own_sem)
+    own.start()
+
+    trial_dms = dms // own_trials
+    band_of = bands * (iota((rows, NSUB), 0) // group) + iota((rows, NSUB), 0) % bands
+    pick = (band_of == iota((rows, NSUB), 1)).astype(bf16)
+    sub = sub_ref[...].astype(f32).astype(bf16)
+    sub = jnp.concatenate([sub, sub], axis=0)
+    delay = lax.dot_general(pick, sub, (((1,), (1,)), ((), ())), preferred_element_type=f32)
+    trial_of = (iota((rows, lanes), 0) % group) // bands
+    same = trial_of == (iota((rows, lanes), 1) % dms) // trial_dms
+    expand(jnp.where(same, delay, -1.0), D2MAX, lanes)
+    below = iota((128, 256), 1) % 128 < iota((128, 256), 0)
+    below = below.astype(f32).astype(bf16)
+
+    def finish_one(step, carry):
+        sending(step).wait()
+        return carry
+
+    own.wait()
+    lax.fori_loop(1, peers, finish_one, 0)
+
+    for start in range(0, block_len, 128):
+        block = incoming[:, :, start:start + 128].reshape(rows, 128)
+        times[start:start + 128, :] = block.astype(f32).T
+    series = shifted_total(D2MAX, lanes)
+    average = jnp.sum(series, axis=0, keepdims=True) / block_len
+    centred = series - average
+    spread = jnp.sum(centred * centred, axis=0, keepdims=True) / block_len
+    deviation = jnp.sqrt(spread + 1e-05)
+    carry = jnp.zeros((1, lanes), f32)
+    for start in range(0, block_len, 128):
+        block = centred[start:start + 128, :]
+        head = block.astype(bf16)
+        tail = (block - head.astype(f32)).astype(bf16)
+        sums = jnp.dot(below, jnp.concatenate([head, tail], axis=0), preferred_element_type=f32) + carry
+        running[start:start + 128, :] = sums
+        carry = sums[127:128, :] + block[127:128, :]
+    after = iota((WMAX, lanes), 0).astype(f32)
+    running[block_len:block_len + WMAX, :] = carry - average * after
+
+    half = block_len // 2
+    left = iota((half + WMAX, lanes), 1) < dms
+    running[0:half + WMAX, :] = jnp.where(left, running[0:half + WMAX, :], running[half:block_len + WMAX, :])
+    base = running[0:half, :]
+    peaks = []
+    for index in range(width_ref.shape[0]):
+        width = width_ref[index]
+        upper = running[pl.ds(width, half), :]
+        peak = jnp.max(upper - base, axis=0, keepdims=True)
+        scale = jnp.sqrt(jnp.full((1, lanes), width.astype(f32)))
+        peaks.append(peak / (deviation * scale))
+    peaks = jnp.concatenate(peaks, axis=0)
+    peaks = jnp.maximum(peaks, pltpu.roll(peaks, dms, 1))
+    out_ref[...] = peaks[:, 0:dms]
+
+
+def fused(data, chan_delay, sub_delay, widths):
+    peers = lax.axis_size("freq")
+    rows, block_len = data.shape
+    bands = rows // CPS
+    dms = sub_delay.shape[0]
+    group = bands * (NSDM // peers)
+    length = block_len + D1MAX + 8
+    wide = (D1MAX // 8 + 1) * NSDM * bands
+    vmem = pl.BlockSpec(memory_space=pltpu.VMEM)
+    peaks = pl.pallas_call(
+        functools.partial(fused_kernel, peers, block_len),
+        out_shape=jax.ShapeDtypeStruct((widths.shape[0], dms), jnp.float32),
+        in_specs=[vmem, vmem, vmem, pl.BlockSpec(memory_space=pltpu.SMEM)],
+        out_specs=vmem,
+        scratch_shapes=[
+            pltpu.VMEM((length + 8, rows), jnp.float32),
+            pltpu.VMEM((length, 8 * rows), jnp.bfloat16),
+            pltpu.VMEM((8 * rows, wide), jnp.bfloat16),
+            pltpu.VMEM((length, wide), jnp.float32),
+            pltpu.VMEM((peers, group, block_len), jnp.bfloat16),
+            pltpu.VMEM((peers, group, block_len), jnp.bfloat16),
+            pltpu.VMEM((block_len + WMAX, 2 * dms), jnp.float32),
+            pltpu.SemaphoreType.DMA((peers,)),
+            pltpu.SemaphoreType.DMA((peers,)),
+            pltpu.SemaphoreType.DMA,
+        ],
+        compiler_params=pltpu.CompilerParams(collective_id=0, has_side_effects=True),
+    )(data, chan_delay, sub_delay, widths)
+    return peaks.T
+
+
 def solution(mesh):
     in_specs = (P(("beam", "freq"), "tm"), P(None, "freq"), P("freq", None), P())
     out_specs = P(("beam", "freq"), None)
+    whole_time = mesh.shape["tm"] == 1
     return jax.shard_map(
-        on_device, mesh=mesh, in_specs=in_specs, out_specs=out_specs, check_vma=False
+        fused if whole_time else on_device, mesh=mesh, in_specs=in_specs, out_specs=out_specs, check_vma=False
     )

time: 114 us -> 16.6 us (0.15)
  loops' own time: 37.8 us -> 0 us
  local copies, waits for them, and re-layouts: 33.8 us -> 1.3 us
  matrix products: 18 us -> 0 us
  blocking collectives: 15.8 us -> 0 us
  Pallas kernels: 0 us -> 15.1 us
  other arithmetic: 6.21 us -> 0 us
  starting transfers between devices: 1.3 us -> 0 us
    another operation x3 -> x0, loops' own time: 37.8 us -> none  [the longest x1 36.5 us: peak_scores(): return lax.map(one_width, widths).T]
    dynamic_update_slice x16 -> x0, local copies, waits for them, and re-layouts: 20.8 us -> none  [peak_scores(): return lax.map(one_width, widths).T]
    dot_general x68 -> x0, matrix products: 18 us -> none  [add_shifts(): jnp.einsum('bsm,bmt->bst', selector, window, preferred_element_type=jnp.f...]
    all_to_all x1 -> x0, blocking collectives: 15.8 us -> none  [on_device(): lax.all_to_all(subband, 'freq', split_axis=1, concat_axis=0, tiled=True)]
    pallas_call x0 -> x1, Pallas kernels: none -> 15.1 us  [fused(): pl.pallas_call(functools.partial(fused_kernel, peers, block_len), out_sha...]
    dynamic_slice x16 -> x0, local copies, waits for them, and re-layouts: 9.2 us -> none  [peak_scores(): return lax.map(one_width, widths).T]
    reduce_max x16 -> x0, other arithmetic: 3.39 us -> none  [one_width(): jnp.max((upper - running[:, :span]) / jnp.sqrt(width.astype(jnp.float32))...]
    another operation x3 -> x0, other arithmetic: 2.24 us -> none
  transfers between devices with their start and end apart: 2 -> 0, of which waited for: 0 -> 0; matrix products, arithmetic and copies ran while one was open for 1% -> 0% of each run, Pallas kernels for 0% -> 0%
where the time goes in v1:
time: 16.6 us; the launch traced here: 16.4 us
  Pallas kernels  15.1 us (91%)
  local copies, waits for them, and re-layouts  1.3 us (8%)
    pallas_call x1, Pallas kernels, fused(): pl.pallas_call(functools.partial(fused_kernel, peers, block_len), out_sha...  15.1 us
    unnamed x1, local copies, waits for them, and re-layouts  1.3 us

profile of v1, /device:TPU:0, one launch (start us, length us, event | category | flops | bytes accessed | tf_op | source)
XLA Modules:
  0.0 16.4 jit_solution(9858459425765262106)
XLA Ops:
  0.0 15.1 %shard_map.46 = f32[16,64]{1,0:T(8,128)} custom-call(bf16[128,640]{1,0:T(8,128)(2,1)} %data_ref.1, s32[64,128]{1,0:T(8,128)} %chan_ref.1, s32[64,64]{1,0:T(8,128)} %sub_ref.1, s32[16]{0:T(128)} %width_ref.1), custom_call_target="tpu_custom_call" | custom-call | tf_op jit(solution)/shard_map/pallas_call | solution.py:228
  15.1 1.3 %copy.6 = f32[64,16]{0,1:T(8,128)} copy(f32[64,16]{0,1:T(8,128)} %bitcast.1) | data formatting | bytes 8192

commit v2 on v1

--- a/solution.py
+++ b/solution.py
@@ -85,8 +85,8 @@
     return lax.pmax(local_peaks, "tm")
 
 
-def fused_kernel(peers, block_len, data_ref, chan_ref, sub_ref, width_ref, out_ref,
-                 times, shifted, select, product, outgoing, incoming,
+def fused_kernel(peers, block_len, data_hbm, chan_hbm, sub_hbm, width_hbm, out_ref,
+                 data_ref, chan_ref, sub_ref, width_ref, load_sem, times, shifted, select, product, outgoing, incoming,
                  running, send_sem, recv_sem, own_sem):
     me = lax.axis_index("freq")
     rows = data_ref.shape[0]
@@ -99,12 +99,24 @@
 
     barrier = pltpu.get_barrier_semaphore()
 
+    def partner(step):
+        if peers & (peers - 1):
+            return lax.rem(me + step, peers)
+        return lax.bitwise_xor(me, peers - step)
+
     def greet(step, carry):
-        pl.semaphore_signal(barrier, inc=1, device_id={"freq": lax.rem(me + step, peers)},
+        pl.semaphore_signal(barrier, inc=1, device_id={"freq": partner(step)},
                             device_id_type=pl.DeviceIdType.MESH)
         return carry
 
     lax.fori_loop(1, peers, greet, 0)
+    loads = [
+        pltpu.make_async_copy(source, target, load_sem.at[index])
+        for index, (source, target) in enumerate((
+            (chan_hbm, chan_ref), (data_hbm, data_ref), (sub_hbm, sub_ref), (width_hbm, width_ref)))
+    ]
+    for load in loads:
+        load.start()
 
     def iota(shape, axis):
         return lax.broadcasted_iota(jnp.int32, shape, axis)
@@ -134,10 +146,12 @@
 
     out_cols = NSDM * bands
     spread = (iota((NSDM, out_cols), 1) // bands == iota((NSDM, out_cols), 0)).astype(bf16)
+    loads[0].wait()
     chan = chan_ref[...].astype(f32).astype(bf16)
     delay = lax.dot_general(chan, spread, (((0,), (0,)), ((), ())), preferred_element_type=f32)
     same = iota((rows, out_cols), 0) // CPS == iota((rows, out_cols), 1) % bands
     expand(jnp.where(same, delay, -1.0), D1MAX, out_cols)
+    loads[1].wait()
     for start in range(0, block_len, 128):
         times[start:start + 128, :] = data_ref[:, start:start + 128].astype(f32).T
     times[block_len:, :] = jnp.zeros((times.shape[0] - block_len, rows), f32)
@@ -150,9 +164,9 @@
 
     def sending(step):
         return pltpu.make_async_remote_copy(
-            src_ref=outgoing.at[lax.rem(me + step, peers)], dst_ref=incoming.at[me],
+            src_ref=outgoing.at[partner(step)], dst_ref=incoming.at[me],
             send_sem=send_sem.at[step], recv_sem=recv_sem.at[step],
-            device_id={"freq": lax.rem(me + step, peers)}, device_id_type=pl.DeviceIdType.MESH)
+            device_id={"freq": partner(step)}, device_id_type=pl.DeviceIdType.MESH)
 
     def start_one(step, carry):
         sending(step).start()
@@ -165,6 +179,8 @@
     trial_dms = dms // own_trials
     band_of = bands * (iota((rows, NSUB), 0) // group) + iota((rows, NSUB), 0) % bands
     pick = (band_of == iota((rows, NSUB), 1)).astype(bf16)
+    loads[2].wait()
+    loads[3].wait()
     sub = sub_ref[...].astype(f32).astype(bf16)
     sub = jnp.concatenate([sub, sub], axis=0)
     delay = lax.dot_general(pick, sub, (((1,), (1,)), ((), ())), preferred_element_type=f32)
@@ -224,13 +240,18 @@
     group = bands * (NSDM // peers)
     length = block_len + D1MAX + 8
     wide = (D1MAX // 8 + 1) * NSDM * bands
-    vmem = pl.BlockSpec(memory_space=pltpu.VMEM)
+    anywhere = pl.BlockSpec(memory_space=pl.ANY)
     peaks = pl.pallas_call(
         functools.partial(fused_kernel, peers, block_len),
-        out_shape=jax.ShapeDtypeStruct((widths.shape[0], dms), jnp.float32),
-        in_specs=[vmem, vmem, vmem, pl.BlockSpec(memory_space=pltpu.SMEM)],
-        out_specs=vmem,
+        out_shape=pltpu.VMEM((widths.shape[0], dms), jnp.float32),
+        in_specs=[anywhere] * 4,
+        out_specs=pl.BlockSpec(memory_space=pltpu.VMEM),
         scratch_shapes=[
+            pltpu.VMEM(data.shape, data.dtype),
+            pltpu.VMEM(chan_delay.shape, chan_delay.dtype),
+            pltpu.VMEM(sub_delay.shape, sub_delay.dtype),
+            pltpu.SMEM(widths.shape, widths.dtype),
+            pltpu.SemaphoreType.DMA((4,)),
             pltpu.VMEM((length + 8, rows), jnp.float32),
             pltpu.VMEM((length, 8 * rows), jnp.bfloat16),
             pltpu.VMEM((8 * rows, wide), jnp.bfloat16),

time: 16.6 us -> 15.7 us (0.946)
  local copies, waits for them, and re-layouts: 1.3 us -> 0.6 us
    unnamed x1, local copies, waits for them, and re-layouts: 1.3 us -> 0.6 us
where the time goes in v2:
time: 15.7 us; the launch traced here: 15.6 us
  Pallas kernels  15 us (96%)
  local copies, waits for them, and re-layouts  0.6 us (4%)
    pallas_call x1, Pallas kernels, fused(): pl.pallas_call(functools.partial(fused_kernel, peers, block_len), out_sha...  15 us
    unnamed x1, local copies, waits for them, and re-layouts  0.6 us

profile of v2, /device:TPU:0, one launch (start us, length us, event | category | flops | bytes accessed | tf_op | source)
XLA Modules:
  0.0 15.6 jit_solution(13039452426131684613)
XLA Ops:
  0.0 15.0 %shard_map.46 = f32[16,64]{1,0:T(8,128)S(1)} custom-call(bf16[128,640]{1,0:T(8,128)(2,1)} %data_hbm.1, s32[64,128]{1,0:T(8,128)} %chan_hbm.1, s32[64,64]{1,0:T(8,128)} %sub_hbm.1, s32[16]{0:T(128)} %width_hbm.1), custom_call_target="tpu_custom_call" | custom-call | tf_op jit(solution)/shard_map/pallas_call | solution.py:244
  15.0 0.6 %copy.6 = f32[64,16]{0,1:T(8,128)} copy(f32[64,16]{0,1:T(8,128)S(1)} %bitcast.1) | data formatting | bytes 8192

commit v3 on v2

--- a/solution.py
+++ b/solution.py
@@ -100,9 +100,7 @@
     barrier = pltpu.get_barrier_semaphore()
 
     def partner(step):
-        if peers & (peers - 1):
-            return lax.rem(me + step, peers)
-        return lax.bitwise_xor(me, peers - step)
+        return lax.rem(me + step, peers)
 
     def greet(step, carry):
         pl.semaphore_signal(barrier, inc=1, device_id={"freq": partner(step)},
@@ -130,7 +128,7 @@
                     block = jnp.where(delay_of == float(8 * high + low), 1.0, 0.0).astype(bf16)
                 select[low * rows:(low + 1) * rows, high * width:(high + 1) * width] = block
 
-    def shifted_total(largest, width):
+    def products(largest, width):
         highs = largest // 8 + 1
         length = block_len + 8 * highs
         for low in range(8):
@@ -139,6 +137,10 @@
             stop = min(start + 128, length)
             product[start:stop, 0:highs * width] = jnp.dot(
                 shifted[start:stop, :], select[:, 0:highs * width], preferred_element_type=f32)
+
+    def shifted_total(largest, width):
+        highs = largest // 8 + 1
+        products(largest, width)
         total = product[0:block_len, 0:width]
         for high in range(1, highs):
             total = total + product[8 * high:8 * high + block_len, high * width:(high + 1) * width]
@@ -182,11 +184,10 @@
     loads[2].wait()
     loads[3].wait()
     sub = sub_ref[...].astype(f32).astype(bf16)
-    sub = jnp.concatenate([sub, sub], axis=0)
     delay = lax.dot_general(pick, sub, (((1,), (1,)), ((), ())), preferred_element_type=f32)
-    trial_of = (iota((rows, lanes), 0) % group) // bands
-    same = trial_of == (iota((rows, lanes), 1) % dms) // trial_dms
-    expand(jnp.where(same, delay, -1.0), D2MAX, lanes)
+    trial_of = (iota((rows, dms), 0) % group) // bands
+    same = trial_of == iota((rows, dms), 1) // trial_dms
+    expand(jnp.where(same, delay, -1.0), D2MAX, dms)
     below = iota((128, 256), 1) % 128 < iota((128, 256), 0)
     below = below.astype(f32).astype(bf16)
 
@@ -200,7 +201,15 @@
     for start in range(0, block_len, 128):
         block = incoming[:, :, start:start + 128].reshape(rows, 128)
         times[start:start + 128, :] = block.astype(f32).T
-    series = shifted_total(D2MAX, lanes)
+    products(D2MAX, dms)
+    pairs = (D2MAX // 8 + 1) // 2
+    mixed = product[0:block_len + 8, 0:lanes]
+    for pair in range(1, pairs):
+        mixed = mixed + product[16 * pair:16 * pair + block_len + 8, pair * lanes:(pair + 1) * lanes]
+    swapped = pltpu.roll(mixed, dms, 1)
+    on_left = iota((block_len, lanes), 1) < dms
+    series = (jnp.where(on_left, mixed[0:block_len], swapped[0:block_len])
+              + jnp.where(on_left, swapped[8:], mixed[8:]))
     average = jnp.sum(series, axis=0, keepdims=True) / block_len
     centred = series - average
     spread = jnp.sum(centred * centred, axis=0, keepdims=True) / block_len

time: 15.7 us -> 14.9 us (0.949)
  Pallas kernels: 15 us -> 14.1 us
    pallas_call x1, Pallas kernels: 15 us -> 14.1 us  [fused(): pl.pallas_call(functools.partial(fused_kernel, peers, block_len), out_sha...]
where the time goes in v3:
time: 14.9 us; the launch traced here: 14.8 us
  Pallas kernels  14.1 us (95%)
  local copies, waits for them, and re-layouts  0.6 us (4%)
    pallas_call x1, Pallas kernels, fused(): pl.pallas_call(functools.partial(fused_kernel, peers, block_len), out_sha...  14.1 us
    unnamed x1, local copies, waits for them, and re-layouts  0.6 us

profile of v3, /device:TPU:0, one launch (start us, length us, event | category | flops | bytes accessed | tf_op | source)
XLA Modules:
  0.0 14.8 jit_solution(16900326877502352933)
XLA Ops:
  0.0 14.1 %shard_map.46 = f32[16,64]{1,0:T(8,128)S(1)} custom-call(bf16[128,640]{1,0:T(8,128)(2,1)} %data_hbm.1, s32[64,128]{1,0:T(8,128)} %chan_hbm.1, s32[64,64]{1,0:T(8,128)} %sub_hbm.1, s32[16]{0:T(128)} %width_hbm.1), custom_call_target="tpu_custom_call" | custom-call | tf_op jit(solution)/shard_map/pallas_call | solution.py:253
  14.2 0.6 %copy.6 = f32[64,16]{0,1:T(8,128)} copy(f32[64,16]{0,1:T(8,128)S(1)} %bitcast.1) | data formatting | bytes 8192

commit v4 on v3

--- a/solution.py
+++ b/solution.py
@@ -133,8 +133,8 @@
         length = block_len + 8 * highs
         for low in range(8):
             shifted[0:length, low * rows:(low + 1) * rows] = times[low:low + length, :].astype(bf16)
-        for start in range(0, length, 128):
-            stop = min(start + 128, length)
+        for start in range(0, length, 352):
+            stop = min(start + 352, length)
             product[start:stop, 0:highs * width] = jnp.dot(
                 shifted[start:stop, :], select[:, 0:highs * width], preferred_element_type=f32)
 

time: 14.9 us -> 14.6 us (0.980)
  Pallas kernels: 14.1 us -> 13.9 us
    pallas_call x1, Pallas kernels: 14.1 us -> 13.9 us  [fused(): pl.pallas_call(functools.partial(fused_kernel, peers, block_len), out_sha...]
where the time goes in v4:
time: 14.6 us; the launch traced here: 14.5 us
  Pallas kernels  13.9 us (95%)
  local copies, waits for them, and re-layouts  0.6 us (4%)
    pallas_call x1, Pallas kernels, fused(): pl.pallas_call(functools.partial(fused_kernel, peers, block_len), out_sha...  13.9 us
    unnamed x1, local copies, waits for them, and re-layouts  0.6 us

profile of v4, /device:TPU:0, one launch (start us, length us, event | category | flops | bytes accessed | tf_op | source)
XLA Modules:
  0.0 14.5 jit_solution(17566271945896490348)
XLA Ops:
  0.0 13.9 %shard_map.46 = f32[16,64]{1,0:T(8,128)S(1)} custom-call(bf16[128,640]{1,0:T(8,128)(2,1)} %data_hbm.1, s32[64,128]{1,0:T(8,128)} %chan_hbm.1, s32[64,64]{1,0:T(8,128)} %sub_hbm.1, s32[16]{0:T(128)} %width_hbm.1), custom_call_target="tpu_custom_call" | custom-call | tf_op jit(solution)/shard_map/pallas_call | solution.py:253
  13.9 0.6 %copy.6 = f32[64,16]{0,1:T(8,128)} copy(f32[64,16]{0,1:T(8,128)S(1)} %bitcast.1) | data formatting | bytes 8192
